TPU v7x, 768 devices: a whole 4x8x12 slice. The times are simulated.
768 devices in a mesh: group: 12 (over z_hi, x), fsdp: 8 (over z_lo, core), tp: 8 (over y).
Axes of the slice: x: 4, y: 8, z: 12 (z_hi: 3, z_lo: 4; z = z_hi * 4 + z_lo), core: 2. Of those that a mesh axis runs over, the one named last changes fastest.
Arguments:
- tokens: bfloat16 [768, 4, 5120], P(('group', 'fsdp')), may hold values from -6 to 6
- queries: bfloat16 [768, 4, 5120], P(('group', 'fsdp'), None, 'tp'), may hold values from -6 to 6
- cache_keys: bfloat16 [768, 512, 1024], P(('group', 'fsdp'), None, 'tp'), may hold values from -6 to 6
- cache_values: bfloat16 [768, 512, 1024], P(('group', 'fsdp'), None, 'tp'), may hold values from -6 to 6
- lengths: int32 [768], P(('group', 'fsdp')), may hold values from 16 to 512, as said below
- weights: float32 [5120, 2048], P(('fsdp', 'tp')), may hold values from -0.078125 to 0.078125
- moment1: float32 [5120, 2048], P(('fsdp', 'tp')), may hold values from -3 to 3
- moment2: float32 [5120, 2048], P(('fsdp', 'tp')), may hold values from 0.25 to 4
- grad_parts: float32 [12, 5120, 2048], P('group', ('fsdp', 'tp')), may hold values from -2 to 2
Outputs:
- new_weights: float32 [5120, 2048], P(('fsdp', 'tp'))
- new_moment1: float32 [5120, 2048], P(('fsdp', 'tp'))
- new_moment2: float32 [5120, 2048], P(('fsdp', 'tp'))
- new_kv: bfloat16 [768, 4, 2048], P(('group', 'fsdp'), None, 'tp')
- context: bfloat16 [768, 4, 5120], P(('group', 'fsdp'), None, 'tp')
Inputs may be any that keep to these rules, and one draw needn't show every extreme that they name: Row r's cache holds lengths[r] valid slots; some row holds 512.
All inputs are finite; a program needn't handle non-finite values.
Results may differ from a plain program's by a relative error of at most 0.0065.
Values may be sent and summed in bfloat16 or wider, within the bound.
A program may use at most 32 MiB of HBM per device.

v0:
```python
import math

import jax
import jax.numpy as jnp
from jax import lax
from jax.sharding import PartitionSpec as P

D = 5120
QH = 40
KVH = 8
HD = 128
STEPS = 4


beta_one = 0.9
beta_two = 0.95
learning_rate = 0.004
decay_rate = 0.1
epsilon = 1e-08
correct_one = 1.0 - 0.9**10
correct_two = 1.0 - 0.95**10
masked_score = -1e30


def adam_update(weights, moment1, moment2, gradient):
    new_moment1 = beta_one * moment1 + (1.0 - beta_one) * gradient
    new_moment2 = beta_two * moment2 + (1.0 - beta_two) * gradient * gradient
    direction = new_moment1 / correct_one / (jnp.sqrt(new_moment2 / correct_two) + epsilon)
    new_weights = weights - learning_rate * (direction + decay_rate * weights)
    return (new_weights, new_moment1, new_moment2)


def rotate_keys(keys, positions):
    half_width = keys.shape[-1] // 2
    frequency = jnp.power(
        jnp.float32(1000000.0), -2.0 * jnp.arange(half_width, dtype=jnp.float32) / keys.shape[-1]
    )
    angles = positions[..., None] * frequency
    leading = keys[..., :half_width]
    trailing = keys[..., half_width:]
    cosine = jnp.cos(angles)
    sine_part = jnp.sin(angles)
    return jnp.concatenate(
        [leading * cosine - trailing * sine_part, trailing * cosine + leading * sine_part], axis=-1
    )


def shards(
    tokens, queries, cache_keys, cache_values, lengths, weights, moment1, moment2, grad_parts
):
    gradient = lax.psum(grad_parts[0], "group")
    new_weights, new_moment1, new_moment2 = adam_update(weights, moment1, moment2, gradient)
    weight_shard = new_weights.astype(jnp.bfloat16)
    tp_count = lax.axis_size("tp")
    fsdp_count = lax.axis_size("fsdp")
    head_cols = weight_shard.shape[1] // tp_count
    row_count = tokens.shape[0]
    token_rows = tokens.reshape(row_count * STEPS, D)
    gathered = lax.all_gather(weight_shard, "fsdp", axis=0, tiled=True)
    spread = lax.all_to_all(gathered, "tp", split_axis=1, concat_axis=0, tiled=True)
    block_rows = weight_shard.shape[0]
    rollout = (
        spread.reshape(tp_count, fsdp_count, block_rows, head_cols)
        .transpose(1, 0, 2, 3)
        .reshape(-1, head_cols)
    )
    projected = jnp.dot(token_rows, rollout, preferred_element_type=jnp.float32)
    kv_heads = head_cols // (2 * HD)
    projected = projected.reshape(row_count, STEPS, kv_heads, 2, HD)
    positions = (lengths[:, None] + jnp.arange(STEPS, dtype=jnp.int32)[None, :]).astype(jnp.float32)
    new_keys = rotate_keys(projected[:, :, :, 0], positions[:, :, None])
    fresh = jnp.stack([new_keys, projected[:, :, :, 1]], axis=3).astype(jnp.bfloat16)
    new_kv = fresh.reshape(row_count, STEPS, head_cols)
    per_group = QH // KVH
    score_scale = 1.0 / math.sqrt(HD)
    span_length = cache_keys.shape[1]
    grouped = queries.reshape(row_count, STEPS, kv_heads, per_group, HD)
    cached_keys = cache_keys.reshape(row_count, span_length, kv_heads, HD)
    cached_values = cache_values.reshape(row_count, span_length, kv_heads, HD)
    new_scores = (
        jnp.einsum(
            "risgd,rjsd->risgj", grouped, fresh[:, :, :, 0], preferred_element_type=jnp.float32
        )
        * score_scale
    )
    causal = jnp.arange(STEPS)[:, None] >= jnp.arange(STEPS)[None, :]
    new_scores = jnp.where(causal[None, :, None, None, :], new_scores, masked_score)
    scores = (
        jnp.einsum("risgd,rpsd->risgp", grouped, cached_keys, preferred_element_type=jnp.float32)
        * score_scale
    )
    in_range = jnp.arange(span_length, dtype=jnp.int32)[None, :] < lengths[:, None]
    all_scores = jnp.concatenate(
        [jnp.where(in_range[:, None, None, None, :], scores, masked_score), new_scores], axis=-1
    )
    highest = jnp.max(all_scores, axis=-1, keepdims=True)
    exponent = jnp.exp(all_scores - highest)
    probs = (exponent / jnp.sum(exponent, axis=-1, keepdims=True)).astype(jnp.bfloat16)
    context = jnp.einsum(
        "risgp,rpsd->risgd",
        probs[..., :span_length],
        cached_values,
        preferred_element_type=jnp.float32,
    )
    context = context + jnp.einsum(
        "risgj,rjsd->risgd",
        probs[..., span_length:],
        fresh[:, :, :, 1],
        preferred_element_type=jnp.float32,
    )
    context = context.reshape(row_count, STEPS, kv_heads * per_group * HD).astype(jnp.bfloat16)
    return (new_weights, new_moment1, new_moment2, new_kv, context)


def solution(mesh):
    in_specs = (
        P(("group", "fsdp"), None, None),
        P(("group", "fsdp"), None, "tp"),
        P(("group", "fsdp"), None, "tp"),
        P(("group", "fsdp"), None, "tp"),
        P(("group", "fsdp")),
        P(("fsdp", "tp"), None),
        P(("fsdp", "tp"), None),
        P(("fsdp", "tp"), None),
        P("group", ("fsdp", "tp"), None),
    )
    out_specs = (
        P(("fsdp", "tp"), None),
        P(("fsdp", "tp"), None),
        P(("fsdp", "tp"), None),
        P(("group", "fsdp"), None, "tp"),
        P(("group", "fsdp"), None, "tp"),
    )
    return jax.shard_map(shards, mesh=mesh, in_specs=in_specs, out_specs=out_specs, check_vma=False)
```

profile of v0, /device:TPU:1, one launch (start us, length us, event | category | flops | bytes accessed | tf_op | source)
XLA Modules:
  0.0 321.6 jit_solution(775488657052040934)
XLA Ops:
  7.2 0.0 copy-start
  7.2 0.0 all-reduce.2.cloned.1.call-start
  7.2 0.7 all-reduce.2.cloned.1.call-update
  7.9 0.0 all-gather.2.cloned.1.call-start
  8.0 168.8 %all-reduce.2.cloned.1.call-done = f32[80,2048]{1,0:T(8,128)} async-done(((f32[80,2048]{1,0:T(8,128)}), f32[80,2048]{1,0:T(8,128)}) %all-reduce.2.cloned.1.call-update) | async-done | bytes 655376 | tf_op jit(solution)/shard_map/psum | solution.py:51
  176.7 3.4 %fusion.20 = (bf16[80,2048]{1,0:T(8,128)(2,1)}, f32[80,2048]{1,0:T(8,128)}, f32[80,2048]{1,0:T(8,128)}, f32[80,2048]{1,0:T(8,128)}) fusion(f32[80,2048]{1,0:T(8,128)} %param.14, f32[80,2048]{1,0:T(8,128)} %all-reduce.2.cloned.1.call-done, f32[80,2048]{1,0:T(8,128)} %param.15, f32[80,2048]{1,0:T(8,128)} %param.16), kind=kLoop, calls=%fused_computation.41 | loop fusion | flops 2621440 | bytes 4915200 | tf_op jit(solution)/shard_map/convert_element_type | solution.py:53
  180.1 0.0 all-gather.2.cloned.1.call-update
  180.1 50.8 %all-gather.2.cloned.1.call-done = bf16[640,2048]{1,0:T(8,128)(2,1)} async-done(((bf16[80,2048]{1,0:T(8,128)(2,1)}), bf16[640,2048]{1,0:T(8,128)(2,1)}) %all-gather.2.cloned.1.call-update) | async-done | bytes 2621456 | tf_op jit(solution)/shard_map/all_gather | solution.py:59
  231.0 4.4 %copy.62 = bf16[640,2048]{0,1:T(8,128)(2,1)} copy(bf16[640,2048]{1,0:T(8,128)(2,1)} %all-gather.2.cloned.1.call-done) | data formatting | bytes 5242880 | tf_op jit(solution)/shard_map/all_gather | solution.py:59
  235.3 6.6 %all-to-all-start = ((bf16[640,8,256]{0,2,1:T(8,128)(2,1)}), bf16[640,8,256]{0,2,1:T(8,128)(2,1)}, u32[]{:S(2)}, u32[]{:S(2)}) async-start(bf16[640,8,256]{0,2,1:T(8,128)(2,1)} %bitcast.83), calls=%async_computation | async-start | bytes 5242880 | tf_op jit(solution)/shard_map/all_to_all | solution.py:60
  241.9 0.0 copy-done.2
  241.9 0.1 reshape.253
  242.0 0.0 copy-done.3
  242.1 0.0 copy-done.4
  242.1 0.1 add_convert_fusion
  242.2 0.1 iota_compare_fusion
  242.2 0.0 copy-done
  242.2 0.5 fusion.23
  242.8 62.2 %all-to-all-done = bf16[640,8,256]{0,2,1:T(8,128)(2,1)} async-done(((bf16[640,8,256]{0,2,1:T(8,128)(2,1)}), bf16[640,8,256]{0,2,1:T(8,128)(2,1)}, u32[]{:S(2)}, u32[]{:S(2)}) %all-to-all-start) | async-done | bytes 2621472 | tf_op jit(solution)/shard_map/all_to_all | solution.py:60
  305.0 4.4 %copy.63 = bf16[8,640,256]{2,1,0:T(8,128)(2,1)} copy(bf16[8,640,256]{1,2,0:T(8,128)(2,1)} %bitcast.2) | data formatting | bytes 5242880 | tf_op jit(solution)/shard_map/all_to_all | solution.py:60
  309.3 1.9 copy.64
  311.3 0.0 copy-start.1
  311.3 0.6 convolution_bitcast_fusion.1
  311.9 0.2 fusion.18
  312.1 0.1 maximum_bitcast_fusion
  312.3 0.2 fusion.24
  312.5 0.3 fusion.12
  312.8 0.2 divide_convert_fusion
  313.0 0.1 fusion.13
  313.2 0.3 fusion.7
  313.5 0.7 reshape.265
  314.1 0.6 reshape.264
  (12 shorter events, 0.1 us)
Async XLA Ops:
  7.2 235.1 %copy-start = (bf16[8,512,128]{2,1,0:T(8,128)(2,1)S(1)}, bf16[8,512,128]{2,1,0:T(8,128)(2,1)}, u32[]{:S(2)}) copy-start(bf16[8,512,128]{2,1,0:T(8,128)(2,1)} %param.11) | copy-start | bytes 3145732
  7.2 169.5 %all-reduce.2.cloned.1.call-start = ((), (), s32[]{:S(2)}) async-start(), calls=%async_computation.1 | async-start | bytes 1310720 | tf_op jit(solution)/shard_map/psum | solution.py:51
  7.9 223.0 %all-gather.2.cloned.1.call-start = ((), (), s32[]{:S(2)}) async-start(), calls=%async_computation.2 | async-start | bytes 2949120 | tf_op jit(solution)/shard_map/all_gather | solution.py:59
  235.3 6.6 %copy-start.2 = (bf16[8,4,5120]{2,1,0:T(4,128)(2,1)S(1)}, bf16[8,4,5120]{2,1,0:T(4,128)(2,1)}, u32[]{:S(2)}) copy-start(bf16[8,4,5120]{2,1,0:T(4,128)(2,1)} %param.9) | copy-start | bytes 983044
  235.3 6.7 %copy-start.3 = (bf16[8,4,640]{2,1,0:T(4,128)(2,1)S(1)}, bf16[8,4,640]{2,1,0:T(4,128)(2,1)}, u32[]{:S(2)}) copy-start(bf16[8,4,640]{2,1,0:T(4,128)(2,1)} %param.10) | copy-start | bytes 122884
  235.3 6.7 %copy-start.4 = (s32[8]{0:T(128)S(1)}, s32[8]{0:T(128)}, u32[]{:S(2)}) copy-start(s32[8]{0:T(128)} %param.13) | copy-start | bytes 100
  235.3 69.6 %all-to-all-start = ((bf16[640,8,256]{0,2,1:T(8,128)(2,1)}), bf16[640,8,256]{0,2,1:T(8,128)(2,1)}, u32[]{:S(2)}, u32[]{:S(2)}) async-start(bf16[640,8,256]{0,2,1:T(8,128)(2,1)} %bitcast.83), calls=%async_computation | async-start | bytes 5242880 | tf_op jit(solution)/shard_map/all_to_all | solution.py:60
  311.3 1.9 copy-start.1
Sparse Core Ops, SparseCore 0:
  11.2 165.4 all-reduce.1
  180.2 50.6 all-gather.1
where the time goes:
time: 322 us
  waiting for transfers between devices  282 us (88%)
  between operations  14.2 us (4%)
  local copies, waits for them, and re-layouts  12.2 us (4%)
  starting transfers between devices  6.66 us (2%)
  other arithmetic  4.34 us (1%)
    psum x1, waiting for transfers between devices, shards(): gradient = lax.psum(grad_parts[0], 'group')  169 us
    all_to_all x1, waiting for transfers between devices, shards(): lax.all_to_all(gathered, 'tp', split_axis=1, concat_axis=0, tiled=True)  62.2 us
    all_gather x1, waiting for transfers between devices, shards(): gathered = lax.all_gather(weight_shard, 'fsdp', axis=0, tiled=True)  50.8 us
    all_to_all x1, starting transfers between devices, shards(): lax.all_to_all(gathered, 'tp', split_axis=1, concat_axis=0, tiled=True)  6.59 us
  transfers between devices with their start and end apart: 3, of which 3 were waited for; matrix products, arithmetic and copies ran while one was open for 0% of the time, Pallas kernels for 0%

commit v1 on v0

--- a/solution.py
+++ b/solution.py
@@ -1,16 +1,19 @@
+import functools
 import math
 
 import jax
 import jax.numpy as jnp
 from jax import lax
+from jax.experimental import pallas as pl
+from jax.experimental.pallas import tpu as pltpu
 from jax.sharding import PartitionSpec as P
 
-D = 5120
 QH = 40
 KVH = 8
 HD = 128
 STEPS = 4
-
+X_CHIPS = 4
+CHUNK = 16
 
 beta_one = 0.9
 beta_two = 0.95
@@ -21,6 +24,8 @@
 correct_two = 1.0 - 0.95**10
 masked_score = -1e30
 
+MESH = pl.DeviceIdType.MESH
+
 
 def adam_update(weights, moment1, moment2, gradient):
     new_moment1 = beta_one * moment1 + (1.0 - beta_one) * gradient
@@ -28,6 +33,242 @@
     direction = new_moment1 / correct_one / (jnp.sqrt(new_moment2 / correct_two) + epsilon)
     new_weights = weights - learning_rate * (direction + decay_rate * weights)
     return (new_weights, new_moment1, new_moment2)
+
+
+def exchange_kernel(
+    nx, nz, nf, nt,
+    grad, weights, moment1, moment2, tokens,
+    new_weights, new_moment1, new_moment2, projected,
+    grad_v, w_v, m1_v, m2_v, gb, xr, zb, gf, wb, wf, tall, pf, pb, pr,
+    grad_sem, in_sem, out_sem, xs, xq, zs, zq, gs, gq, ys, yq, ts, tq, ps, pq,
+):
+    group = lax.axis_index("group")
+    f = lax.axis_index("fsdp")
+    t = lax.axis_index("tp")
+    x = lax.rem(group, nx)
+    z = lax.div(group, nx)
+    rows_all = grad_v.shape[0]
+    cx = gb.shape[2]
+    hc = wf.shape[2]
+    depth = tall.shape[2]
+    chunks = rows_all // CHUNK
+
+    x_to = [z * nx + lax.rem(x + d, nx) for d in range(nx)]
+    z_to = [lax.rem(z + d, nz) * nx + x for d in range(nz)]
+    f_at = [lax.rem(f + d, nf) for d in range(nf)]
+    t_at = [lax.rem(t + d, nt) for d in range(nt)]
+    x_from = [lax.rem(x + nx - d, nx) for d in range(nx)]
+    z_from = [lax.rem(z + nz - d, nz) for d in range(nz)]
+    f_from = [lax.rem(f + nf - d, nf) for d in range(nf)]
+    t_from = [lax.rem(t + nt - d, nt) for d in range(nt)]
+
+    barrier = pltpu.get_barrier_semaphore()
+    peers = (
+        [(x_to[d], f, t) for d in range(1, nx)]
+        + [(z_to[d], f, t) for d in range(1, nz)]
+        + [(group, f, t_at[d]) for d in range(1, nt)]
+        + [(group, f_at[d], t) for d in range(1, nf)]
+    )
+    for peer in peers:
+        pl.semaphore_signal(barrier, inc=1, device_id=peer, device_id_type=MESH)
+
+    def rows_of(r):
+        return pl.ds(r * CHUNK, CHUNK)
+
+    loads = [
+        pltpu.make_async_copy(grad.at[0, rows_of(r)], grad_v.at[rows_of(r)], grad_sem.at[r])
+        for r in range(chunks)
+    ]
+    for load in loads:
+        load.start()
+    own_tokens = pltpu.make_async_copy(
+        tokens.at[:, pl.ds(pl.multiple_of(f * depth, 128), depth)], tall.at[f], in_sem.at[3]
+    )
+    own_tokens.start()
+    state = [
+        pltpu.make_async_copy(src, dst, in_sem.at[i])
+        for i, (src, dst) in enumerate(((weights, w_v), (moment1, m1_v), (moment2, m2_v)))
+    ]
+    for load in state:
+        load.start()
+
+    def cast(r):
+        loads[r].wait()
+        for i in range(nx):
+            gb[i, rows_of(r)] = grad_v[rows_of(r), pl.ds(i * cx, cx)].astype(jnp.bfloat16)
+
+    def remote(src, dst, send, recv, device):
+        return pltpu.make_async_remote_copy(
+            src_ref=src, dst_ref=dst, send_sem=send, recv_sem=recv,
+            device_id=device, device_id_type=MESH,
+        )
+
+    started = []
+
+    def send(*args):
+        copy = remote(*args)
+        copy.start()
+        started.append(copy)
+
+    def arrive(dst, send_sem, recv_sem):
+        remote(dst, dst, send_sem, recv_sem, (group, f, t)).wait_recv()
+
+    def scatter_x(r):
+        for d in range(1, nx):
+            send(
+                gb.at[lax.rem(x + d, nx), rows_of(r)], xr.at[d - 1, rows_of(r)],
+                xs.at[r, d - 1], xq.at[r, d - 1], (x_to[d], f, t),
+            )
+
+    def exchange_z(r):
+        total = gb[x, rows_of(r)].astype(jnp.float32)
+        for d in range(1, nx):
+            arrive(xr.at[d - 1, rows_of(r)], xs.at[r, d - 1], xq.at[r, d - 1])
+            total += xr[d - 1, rows_of(r)].astype(jnp.float32)
+        zb[z, rows_of(r)] = total.astype(jnp.bfloat16)
+        for d in range(1, nz):
+            send(
+                zb.at[z, rows_of(r)], zb.at[z, rows_of(r)],
+                zs.at[r, d - 1], zq.at[r, d - 1], (z_to[d], f, t),
+            )
+
+    def gather_x(r):
+        for d in range(1, nz):
+            arrive(zb.at[z_from[d], rows_of(r)], zs.at[r, d - 1], zq.at[r, d - 1])
+        total = zb[0, rows_of(r)].astype(jnp.float32)
+        for i in range(1, nz):
+            total += zb[i, rows_of(r)].astype(jnp.float32)
+        gf[x, rows_of(r)] = total.astype(jnp.bfloat16)
+        for d in range(1, nx):
+            send(
+                gf.at[x, rows_of(r)], gf.at[x, rows_of(r)],
+                gs.at[r, d - 1], gq.at[r, d - 1], (x_to[d], f, t),
+            )
+
+    t_order = sorted(range(1, nt), key=lambda d: -min(d, nt - d))
+
+    def update(r):
+        for d in range(1, nx):
+            arrive(gf.at[x_from[d], rows_of(r)], gs.at[r, d - 1], gq.at[r, d - 1])
+        for i in range(nx):
+            columns = pl.ds(i * cx, cx)
+            new_w, new_1, new_2 = adam_update(
+                w_v[rows_of(r), columns],
+                m1_v[rows_of(r), columns],
+                m2_v[rows_of(r), columns],
+                gf[i, rows_of(r)].astype(jnp.float32),
+            )
+            w_v[rows_of(r), columns] = new_w
+            m1_v[rows_of(r), columns] = new_1
+            m2_v[rows_of(r), columns] = new_2
+            rounded = new_w.astype(jnp.bfloat16)
+            for j in range(cx // hc):
+                wb[i * (cx // hc) + j, rows_of(r)] = rounded[:, j * hc : (j + 1) * hc]
+        for d in t_order:
+            send(
+                wb.at[t_at[d], rows_of(r)], wf.at[t, rows_of(r)],
+                ys.at[r, d - 1], yq.at[r, d - 1], (group, f, t_at[d]),
+            )
+        wf[t, rows_of(r)] = wb[t, rows_of(r)]
+
+    for r in range(chunks):
+        cast(r)
+    pl.semaphore_wait(barrier, len(peers))
+    for r in range(chunks):
+        scatter_x(r)
+    for r in range(chunks):
+        exchange_z(r)
+    for d in range(1, nf):
+        send(
+            tokens.at[:, pl.ds(pl.multiple_of(f_at[d] * depth, 128), depth)], tall.at[f],
+            ts.at[d - 1], tq.at[d - 1], (group, f_at[d], t),
+        )
+    for load in state:
+        load.wait()
+    gather_x(0)
+    for r in range(1, chunks):
+        gather_x(r)
+        update(r - 1)
+    update(chunks - 1)
+
+    stores = [
+        pltpu.make_async_copy(src, dst, out_sem.at[i])
+        for i, (src, dst) in enumerate(
+            ((w_v, new_weights), (m1_v, new_moment1), (m2_v, new_moment2))
+        )
+    ]
+    for store in stores:
+        store.start()
+
+    own_tokens.wait()
+    for d in range(1, nf):
+        arrive(tall.at[f_from[d]], ts.at[d - 1], tq.at[d - 1])
+    for r in range(chunks):
+        for d in range(1, nt):
+            arrive(wf.at[t_from[d], rows_of(r)], ys.at[r, d - 1], yq.at[r, d - 1])
+    partial = jnp.dot(
+        tall[...].reshape(-1, depth), wf[...].reshape(depth, hc), preferred_element_type=jnp.float32
+    ).reshape(pf.shape)
+    pb[...] = partial.astype(jnp.bfloat16)
+    for d in range(1, nf):
+        send(
+            pb.at[f_at[d]], pr.at[f], ps.at[d - 1], pq.at[d - 1], (group, f_at[d], t)
+        )
+    pf[...] = partial
+    total = pf[f]
+    for d in range(1, nf):
+        arrive(pr.at[f_from[d]], ps.at[d - 1], pq.at[d - 1])
+        total += pr[f_from[d]].astype(jnp.float32)
+    projected[...] = total
+    for copy in started:
+        copy.wait_send()
+    for store in stores:
+        store.wait()
+
+
+def exchange(sizes, grad_parts, weights, moment1, moment2, tokens):
+    nx, nz, nf, nt = sizes
+    rows, columns = weights.shape
+    token_rows = tokens.shape[0]
+    cx = columns // nx
+    hc = columns // nt
+    depth = nt * rows
+    chunks = rows // CHUNK
+    dma = pltpu.SemaphoreType.DMA
+    f32 = jnp.float32
+    bf16 = jnp.bfloat16
+    any_space = pl.BlockSpec(memory_space=pl.ANY)
+    return pl.pallas_call(
+        functools.partial(exchange_kernel, nx, nz, nf, nt),
+        out_shape=[jax.ShapeDtypeStruct((rows, columns), f32)] * 3
+        + [jax.ShapeDtypeStruct((token_rows, hc), f32)],
+        in_specs=[any_space] * 5,
+        out_specs=[any_space] * 3 + [pl.BlockSpec(memory_space=pltpu.VMEM)],
+        scratch_shapes=[pltpu.VMEM((rows, columns), f32)] * 4
+        + [
+            pltpu.VMEM((nx, rows, cx), bf16),
+            pltpu.VMEM((nx - 1, rows, cx), bf16),
+            pltpu.VMEM((nz, rows, cx), bf16),
+            pltpu.VMEM((nx, rows, cx), bf16),
+            pltpu.VMEM((nt, rows, hc), bf16),
+            pltpu.VMEM((nt, rows, hc), bf16),
+            pltpu.VMEM((nf, token_rows, depth), bf16),
+            pltpu.VMEM((nf, token_rows, hc), f32),
+            pltpu.VMEM((nf, token_rows, hc), bf16),
+            pltpu.VMEM((nf, token_rows, hc), bf16),
+            dma((chunks,)),
+            dma((4,)),
+            dma((3,)),
+        ]
+        + [dma((chunks, nx - 1))] * 2
+        + [dma((chunks, nz - 1))] * 2
+        + [dma((chunks, nx - 1))] * 2
+        + [dma((chunks, nt - 1))] * 2
+        + [dma((nf - 1,))] * 4,
+        compiler_params=pltpu.CompilerParams(
+            collective_id=0, has_side_effects=True, vmem_limit_bytes=32 << 20
+        ),
+    )(grad_parts, weights, moment1, moment2, tokens)
 
 
 def rotate_keys(keys, positions):
@@ -46,25 +287,14 @@
 
 
 def shards(
-    tokens, queries, cache_keys, cache_values, lengths, weights, moment1, moment2, grad_parts
+    sizes, tokens, queries, cache_keys, cache_values, lengths, weights, moment1, moment2, grad_parts
 ):
-    gradient = lax.psum(grad_parts[0], "group")
-    new_weights, new_moment1, new_moment2 = adam_update(weights, moment1, moment2, gradient)
-    weight_shard = new_weights.astype(jnp.bfloat16)
-    tp_count = lax.axis_size("tp")
-    fsdp_count = lax.axis_size("fsdp")
-    head_cols = weight_shard.shape[1] // tp_count
     row_count = tokens.shape[0]
-    token_rows = tokens.reshape(row_count * STEPS, D)
-    gathered = lax.all_gather(weight_shard, "fsdp", axis=0, tiled=True)
-    spread = lax.all_to_all(gathered, "tp", split_axis=1, concat_axis=0, tiled=True)
-    block_rows = weight_shard.shape[0]
-    rollout = (
-        spread.reshape(tp_count, fsdp_count, block_rows, head_cols)
-        .transpose(1, 0, 2, 3)
-        .reshape(-1, head_cols)
-    )
-    projected = jnp.dot(token_rows, rollout, preferred_element_type=jnp.float32)
+    token_rows = tokens.reshape(row_count * STEPS, tokens.shape[2])
+    new_weights, new_moment1, new_moment2, projected = exchange(
+        sizes, grad_parts, weights, moment1, moment2, token_rows
+    )
+    head_cols = projected.shape[1]
     kv_heads = head_cols // (2 * HD)
     projected = projected.reshape(row_count, STEPS, kv_heads, 2, HD)
     positions = (lengths[:, None] + jnp.arange(STEPS, dtype=jnp.int32)[None, :]).astype(jnp.float32)
@@ -131,4 +361,12 @@
         P(("group", "fsdp"), None, "tp"),
         P(("group", "fsdp"), None, "tp"),
     )
-    return jax.shard_map(shards, mesh=mesh, in_specs=in_specs, out_specs=out_specs, check_vma=False)
+    nx = X_CHIPS
+    sizes = (nx, mesh.shape["group"] // nx, mesh.shape["fsdp"], mesh.shape["tp"])
+    return jax.shard_map(
+        functools.partial(shards, sizes),
+        mesh=mesh,
+        in_specs=in_specs,
+        out_specs=out_specs,
+        check_vma=False,
+    )

time: 322 us -> 66.7 us (0.21)
  waiting for transfers between devices: 282 us -> 0 us
  Pallas kernels: 0 us -> 52.1 us
  between operations: 14.2 us -> 0.75 us
  starting transfers between devices: 6.66 us -> 0 us
  other arithmetic: 4.34 us -> 0.95 us
    psum x1 -> x0, waiting for transfers between devices: 169 us -> none  [shards(): gradient = lax.psum(grad_parts[0], 'group')]
    all_to_all x1 -> x0, waiting for transfers between devices: 62.2 us -> none  [shards(): lax.all_to_all(gathered, 'tp', split_axis=1, concat_axis=0, tiled=True)]
    pallas_call x0 -> x1, Pallas kernels: none -> 52.1 us  [exchange(): pl.pallas_call(functools.partial(exchange_kernel, nx, nz, nf, nt), out_sh...]
    all_gather x1 -> x0, waiting for transfers between devices: 50.8 us -> none  [shards(): gathered = lax.all_gather(weight_shard, 'fsdp', axis=0, tiled=True)]
    unnamed x12 -> x21, local copies, waits for them, and re-layouts: 0.66 us -> 9.4 us
    all_to_all x1 -> x0, starting transfers between devices: 6.59 us -> none  [shards(): lax.all_to_all(gathered, 'tp', split_axis=1, concat_axis=0, tiled=True)]
    all_gather x1 -> x0, local copies, waits for them, and re-layouts: 4.38 us -> none  [shards(): gathered = lax.all_gather(weight_shard, 'fsdp', axis=0, tiled=True)]
    all_to_all x1 -> x0, local copies, waits for them, and re-layouts: 4.38 us -> none  [shards(): lax.all_to_all(gathered, 'tp', split_axis=1, concat_axis=0, tiled=True)]
  transfers between devices with their start and end apart: 3 -> 0, of which waited for: 3 -> 0; matrix products, arithmetic and copies ran while one was open for 0% -> 0% of each run, Pallas kernels for 0% -> 0%
where the time goes in v1:
time: 66.7 us; the launch traced here: 66.3 us
  Pallas kernels  52.1 us (78%)
  local copies, waits for them, and re-layouts  11.3 us (17%)
  matrix products  1.23 us (2%)
  other arithmetic  0.95 us (1%)
  between operations  0.75 us (1%)
    pallas_call x1, Pallas kernels, exchange(): pl.pallas_call(functools.partial(exchange_kernel, nx, nz, nf, nt), out_sh...  52.1 us
    unnamed x21, local copies, waits for them, and re-layouts  9.4 us

profile of v1, /device:TPU:1, one launch (start us, length us, event | category | flops | bytes accessed | tf_op | source)
XLA Modules:
  0.0 66.3 jit_solution(2602545456854314068)
XLA Ops:
  0.6 0.0 copy-start
  0.6 1.1 %reshape.241.tokens = bf16[32,5120]{1,0:T(8,128)(2,1)S(1)} reshape(bf16[8,4,5120]{2,1,0:T(4,128)(2,1)} %param.9) | data formatting | bytes 655360 | tf_op jit(solution)/shard_map/reshape | solution.py:293
  1.8 0.0 copy-start.1
  1.8 1.1 %copy-done.1 = f32[1,80,2048]{2,1,0:T(8,128)S(1)} copy-done((f32[1,80,2048]{2,1,0:T(8,128)S(1)}, f32[1,80,2048]{2,1,0:T(8,128)}, u32[]{:S(2)}) %copy-start.1) | copy-done | bytes 655384
  2.9 0.0 copy-start.2
  2.9 1.1 %copy-done.2 = f32[80,2048]{1,0:T(8,128)S(1)} copy-done((f32[80,2048]{1,0:T(8,128)S(1)}, f32[80,2048]{1,0:T(8,128)}, u32[]{:S(2)}) %copy-start.2) | copy-done | bytes 655384
  4.0 0.0 copy-start.3
  4.0 1.1 %copy-done.3 = f32[80,2048]{1,0:T(8,128)S(1)} copy-done((f32[80,2048]{1,0:T(8,128)S(1)}, f32[80,2048]{1,0:T(8,128)}, u32[]{:S(2)}) %copy-start.3) | copy-done | bytes 655384
  5.1 0.0 copy-start.4
  5.1 1.1 %copy-done.4 = f32[80,2048]{1,0:T(8,128)S(1)} copy-done((f32[80,2048]{1,0:T(8,128)S(1)}, f32[80,2048]{1,0:T(8,128)}, u32[]{:S(2)}) %copy-start.4) | copy-done | bytes 655384
  6.1 52.1 %shard_map.128 = (f32[80,2048]{1,0:T(8,128)S(1)}, f32[80,2048]{1,0:T(8,128)S(1)}, f32[80,2048]{1,0:T(8,128)S(1)}, f32[32,256]{1,0:T(8,128)S(1)}) custom-call(f32[1,80,2048]{2,1,0:T(8,128)S(1)} %copy-done.1, f32[80,2048]{1,0:T(8,128)S(1)} %copy-done.2, f32[80,2048]{1,0:T(8,128)S(1)} %copy-done.3, f32[80,2048]{1,0:T(8,128)S(1)} %copy-done.4, ...), custom_call_target="tpu_custom_call" | custom-call | tf_op jit(solution)/shard_map/pallas_call | solution.py:241
  58.3 0.0 copy-start.7
  58.3 0.6 copy-done.7
  59.0 0.1 add_convert_fusion
  59.1 0.2 fusion.17
  59.3 0.0 copy-start.6
  59.3 0.1 maximum_bitcast_fusion
  59.4 0.7 %copy-done.6 = bf16[8,4,640]{2,1,0:T(4,128)(2,1)S(1)} copy-done((bf16[8,4,640]{2,1,0:T(4,128)(2,1)S(1)}, bf16[8,4,640]{2,1,0:T(4,128)(2,1)}, u32[]{:S(2)}) %copy-start.6) | copy-done | bytes 40984
  60.1 0.2 fusion.21
  60.3 0.1 iota_compare_fusion
  60.4 0.0 copy-done
  60.4 0.5 fusion.20
  61.0 0.3 fusion.11
  61.3 0.2 divide_convert_fusion
  61.5 0.1 fusion.12
  61.6 0.6 copy-done.5
  62.2 0.3 fusion.7
  62.5 0.7 reshape.253
  63.2 0.6 reshape.252
  63.8 0.8 %copy.44 = f32[80,2048]{1,0:T(8,128)} copy(f32[80,2048]{1,0:T(8,128)S(1)} %get-tuple-element.31) | data formatting | bytes 1310720
  64.6 0.8 %copy.45 = f32[80,2048]{1,0:T(8,128)} copy(f32[80,2048]{1,0:T(8,128)S(1)} %get-tuple-element.32) | data formatting | bytes 1310720
  65.5 0.8 %copy.46 = f32[80,2048]{1,0:T(8,128)} copy(f32[80,2048]{1,0:T(8,128)S(1)} %get-tuple-element.33) | data formatting | bytes 1310720
  (9 shorter events, 0.1 us)
Async XLA Ops:
  0.6 59.8 %copy-start = (bf16[8,512,128]{2,1,0:T(8,128)(2,1)S(1)}, bf16[8,512,128]{2,1,0:T(8,128)(2,1)}, u32[]{:S(2)}) copy-start(bf16[8,512,128]{2,1,0:T(8,128)(2,1)} %param.11) | copy-start | bytes 3145732
  1.8 1.1 %copy-start.1 = (f32[1,80,2048]{2,1,0:T(8,128)S(1)}, f32[1,80,2048]{2,1,0:T(8,128)}, u32[]{:S(2)}) copy-start(f32[1,80,2048]{2,1,0:T(8,128)} %grad.1) | copy-start | bytes 1966084
  2.9 1.1 %copy-start.2 = (f32[80,2048]{1,0:T(8,128)S(1)}, f32[80,2048]{1,0:T(8,128)}, u32[]{:S(2)}) copy-start(f32[80,2048]{1,0:T(8,128)} %weights.1) | copy-start | bytes 1966084
  4.0 1.1 %copy-start.3 = (f32[80,2048]{1,0:T(8,128)S(1)}, f32[80,2048]{1,0:T(8,128)}, u32[]{:S(2)}) copy-start(f32[80,2048]{1,0:T(8,128)} %moment1.1) | copy-start | bytes 1966084
  5.1 1.1 %copy-start.4 = (f32[80,2048]{1,0:T(8,128)S(1)}, f32[80,2048]{1,0:T(8,128)}, u32[]{:S(2)}) copy-start(f32[80,2048]{1,0:T(8,128)} %moment2.1) | copy-start | bytes 1966084
  58.3 0.7 copy-start.7
  59.3 0.8 %copy-start.6 = (bf16[8,4,640]{2,1,0:T(4,128)(2,1)S(1)}, bf16[8,4,640]{2,1,0:T(4,128)(2,1)}, u32[]{:S(2)}) copy-start(bf16[8,4,640]{2,1,0:T(4,128)(2,1)} %param.10) | copy-start | bytes 122884
  61.0 1.2 %copy-start.5 = (bf16[8,512,128]{2,1,0:T(8,128)(2,1)S(1)}, bf16[8,512,128]{2,1,0:T(8,128)(2,1)}, u32[]{:S(2)}) copy-start(bf16[8,512,128]{2,1,0:T(8,128)(2,1)} %param.12) | copy-start | bytes 3145732

commit v2 on v1

v2 whole, which is shorter than its diff:
```python
import functools
import math

import jax
import jax.numpy as jnp
from jax import lax
from jax.experimental import pallas as pl
from jax.experimental.pallas import tpu as pltpu
from jax.sharding import PartitionSpec as P

QH = 40
KVH = 8
HD = 128
STEPS = 4
X_CHIPS = 4
CHUNK = 16

beta_one = 0.9
beta_two = 0.95
learning_rate = 0.004
decay_rate = 0.1
epsilon = 1e-08
correct_one = 1.0 - 0.9**10
correct_two = 1.0 - 0.95**10
masked_score = -1e30
SCORE_SCALE = 1.0 / math.sqrt(HD)

MESH = pl.DeviceIdType.MESH


def adam_update(weights, moment1, moment2, gradient):
    new_moment1 = beta_one * moment1 + (1.0 - beta_one) * gradient
    new_moment2 = beta_two * moment2 + (1.0 - beta_two) * gradient * gradient
    direction = new_moment1 / correct_one / (jnp.sqrt(new_moment2 / correct_two) + epsilon)
    new_weights = weights - learning_rate * (direction + decay_rate * weights)
    return (new_weights, new_moment1, new_moment2)


def exchange_kernel(
    nx, nz, nf, nt,
    grad, weights, moment1, moment2, tokens, queries, cache_keys, cache_values, lengths,
    new_w, new_1, new_2, projected, query_rows, top, mass, cached, cosine, sine,
    grad_v, w_v, m1_v, m2_v, tok_v, q_v, k_v, v_v, len_s, row_v, tb, qf,
    gb, xr, zb, gf, wb, wf, tall, pf, pb, pr,
    grad_sem, in_sem, xs, xq, zs, zq, gs, gq, ys, yq, ts, tq, ps, pq,
):
    group = lax.axis_index("group")
    f = lax.axis_index("fsdp")
    t = lax.axis_index("tp")
    x = lax.rem(group, nx)
    z = lax.div(group, nx)
    rows_all = grad_v.shape[0]
    cx = gb.shape[2]
    hc = wf.shape[2]
    depth = tall.shape[2]
    chunks = rows_all // CHUNK
    f32 = jnp.float32
    bf16 = jnp.bfloat16

    x_to = [z * nx + lax.rem(x + d, nx) for d in range(nx)]
    z_to = [lax.rem(z + d, nz) * nx + x for d in range(nz)]
    f_at = [lax.rem(f + d, nf) for d in range(nf)]
    t_at = [lax.rem(t + d, nt) for d in range(nt)]
    x_from = [lax.rem(x + nx - d, nx) for d in range(nx)]
    z_from = [lax.rem(z + nz - d, nz) for d in range(nz)]
    f_from = [lax.rem(f + nf - d, nf) for d in range(nf)]
    t_from = [lax.rem(t + nt - d, nt) for d in range(nt)]

    barrier = pltpu.get_barrier_semaphore()
    peers = (
        [(z_to[d], f, t) for d in range(1, nz)]
        + [(group, f, t_at[d]) for d in range(1, nt)]
        + [(group, f_at[d], t) for d in range(1, nf)]
        + [(x_to[d], f, t) for d in range(1, nx)]
    )
    for peer in peers:
        pl.semaphore_signal(barrier, inc=1, device_id=peer, device_id_type=MESH)

    def rows_of(r):
        return pl.ds(r * CHUNK, CHUNK)

    loads = [
        pltpu.make_async_copy(grad.at[0, rows_of(r)], grad_v.at[rows_of(r)], grad_sem.at[r])
        for r in range(chunks)
    ]
    others = [
        pltpu.make_async_copy(src, dst, in_sem.at[i])
        for i, (src, dst) in enumerate(
            (
                (tokens, tok_v), (queries, q_v), (lengths, len_s), (cache_keys, k_v),
                (cache_values, v_v), (weights, w_v), (moment1, m1_v), (moment2, m2_v),
            )
        )
    ]
    for load in loads + others:
        load.start()

    def cast(r):
        loads[r].wait()
        for i in range(nx):
            gb[i, rows_of(r)] = grad_v[rows_of(r), pl.ds(i * cx, cx)].astype(bf16)

    def remote(src, dst, send, recv, device):
        return pltpu.make_async_remote_copy(
            src_ref=src, dst_ref=dst, send_sem=send, recv_sem=recv,
            device_id=device, device_id_type=MESH,
        )

    started = []

    def send(*args):
        copy = remote(*args)
        copy.start()
        started.append(copy)

    def arrive(dst, send_sem, recv_sem):
        remote(dst, dst, send_sem, recv_sem, (group, f, t)).wait_recv()

    def scatter_x(r):
        for d in range(1, nx):
            send(
                gb.at[lax.rem(x + d, nx), rows_of(r)], xr.at[d - 1, rows_of(r)],
                xs.at[r, d - 1], xq.at[r, d - 1], (x_to[d], f, t),
            )

    def exchange_z(r):
        total = gb[x, rows_of(r)].astype(f32)
        for d in range(1, nx):
            arrive(xr.at[d - 1, rows_of(r)], xs.at[r, d - 1], xq.at[r, d - 1])
            total += xr[d - 1, rows_of(r)].astype(f32)
        zb[z, rows_of(r)] = total.astype(bf16)
        for d in range(1, nz):
            send(
                zb.at[z, rows_of(r)], zb.at[z, rows_of(r)],
                zs.at[r, d - 1], zq.at[r, d - 1], (z_to[d], f, t),
            )

    def gather_x(r):
        for d in range(1, nz):
            arrive(zb.at[z_from[d], rows_of(r)], zs.at[r, d - 1], zq.at[r, d - 1])
        total = zb[0, rows_of(r)].astype(f32)
        for i in range(1, nz):
            total += zb[i, rows_of(r)].astype(f32)
        gf[x, rows_of(r)] = total.astype(bf16)
        for d in range(1, nx):
            send(
                gf.at[x, rows_of(r)], gf.at[x, rows_of(r)],
                gs.at[r, d - 1], gq.at[r, d - 1], (x_to[d], f, t),
            )

    t_order = sorted(range(1, nt), key=lambda d: -min(d, nt - d))

    def update(r):
        for d in range(1, nx):
            arrive(gf.at[x_from[d], rows_of(r)], gs.at[r, d - 1], gq.at[r, d - 1])
        for i in range(nx):
            columns = pl.ds(i * cx, cx)
            w, one, two = adam_update(
                w_v[rows_of(r), columns],
                m1_v[rows_of(r), columns],
                m2_v[rows_of(r), columns],
                gf[i, rows_of(r)].astype(f32),
            )
            new_w[rows_of(r), columns] = w
            new_1[rows_of(r), columns] = one
            new_2[rows_of(r), columns] = two
            rounded = w.astype(bf16)
            for j in range(cx // hc):
                wb[i * (cx // hc) + j, rows_of(r)] = rounded[:, j * hc : (j + 1) * hc]
        for d in t_order:
            send(
                wb.at[t_at[d], rows_of(r)], wf.at[t, rows_of(r)],
                ys.at[r, d - 1], yq.at[r, d - 1], (group, f, t_at[d]),
            )
        wf[t, rows_of(r)] = wb[t, rows_of(r)]

    def lay_out_tokens():
        others[0].wait()
        for i in range(nf):
            for row in range(tok_v.shape[0]):
                row_v[pl.ds(row * STEPS, STEPS)] = tok_v[row, :, pl.ds(i * depth, depth)].astype(f32)
            tb[i] = row_v[...].astype(bf16)
        tall[f] = tb[f]

    def attend_cache():
        for load in others[1:5]:
            load.wait()
        heads = QH // KVH
        qf[:, pl.ds(heads * STEPS, 4)] = jnp.zeros((qf.shape[0], 4, HD), f32)
        for head in range(heads):
            qf[:, pl.ds(head * STEPS, STEPS)] = q_v[:, :, pl.ds(head * HD, HD)].astype(f32)
        pad = qf.shape[1]
        query_rows[...] = qf[...].reshape(-1, HD).astype(bf16)
        slots = lax.broadcasted_iota(jnp.int32, (pad, k_v.shape[1]), 1)
        for row in range(qf.shape[0]):
            scores = lax.dot_general(
                qf[row].astype(bf16), k_v[row], (((1,), (1,)), ((), ())),
                preferred_element_type=f32,
            ) * SCORE_SCALE
            scores = jnp.where(slots < len_s[row], scores, masked_score)
            highest = jnp.max(scores, axis=-1, keepdims=True)
            exponent = jnp.exp(scores - highest)
            out = pl.ds(row * pad, pad)
            top[out] = jnp.broadcast_to(highest, (pad, HD))
            mass[out] = jnp.broadcast_to(jnp.sum(exponent, axis=-1, keepdims=True), (pad, HD))
            cached[out] = jnp.dot(exponent.astype(bf16), v_v[row], preferred_element_type=f32)
        token_rows = qf.shape[0] * STEPS
        at = lax.broadcasted_iota(jnp.int32, (token_rows, HD), 0)
        lane = lax.broadcasted_iota(jnp.int32, (token_rows, HD), 1)
        position = lax.rem(at, STEPS)
        for row in range(qf.shape[0]):
            position += jnp.where(lax.div(at, STEPS) == row, len_s[row], 0)
        power = lax.rem(lane, HD // 2).astype(f32) * (-2.0 / HD)
        angle = position.astype(f32) * jnp.exp(power * math.log(1000000.0))
        cosine[...] = jnp.cos(angle)
        turn = jnp.sin(angle)
        sine[...] = jnp.where(lane < HD // 2, -turn, turn)

    for r in range(chunks):
        cast(r)
    pl.semaphore_wait(barrier, len(peers))
    for r in range(chunks):
        scatter_x(r)
    lay_out_tokens()
    attend_cache()
    for r in range(chunks):
        exchange_z(r)
    for d in range(1, nf):
        send(tb.at[f_at[d]], tall.at[f], ts.at[d - 1], tq.at[d - 1], (group, f_at[d], t))
    for load in others[5:]:
        load.wait()
    gather_x(0)
    for r in range(1, chunks):
        gather_x(r)
        update(r - 1)
    update(chunks - 1)

    for d in range(1, nf):
        arrive(tall.at[f_from[d]], ts.at[d - 1], tq.at[d - 1])
    for r in range(chunks):
        for d in range(1, nt):
            arrive(wf.at[t_from[d], rows_of(r)], ys.at[r, d - 1], yq.at[r, d - 1])
    partial = jnp.dot(
        tall[...].reshape(-1, depth), wf[...].reshape(depth, hc), preferred_element_type=f32
    ).reshape(pf.shape)
    pb[...] = partial.astype(bf16)
    for d in range(1, nf):
        send(pb.at[f_at[d]], pr.at[f], ps.at[d - 1], pq.at[d - 1], (group, f_at[d], t))
    pf[...] = partial
    total = pf[f]
    for d in range(1, nf):
        arrive(pr.at[f_from[d]], ps.at[d - 1], pq.at[d - 1])
        total += pr[f_from[d]].astype(f32)
    projected[...] = total
    for copy in started:
        copy.wait_send()


def finish_kernel(
    new_w, new_1, new_2, projected, query_rows, top, mass, cached, cosine, sine,
    w_out, m1_out, m2_out, kv_out, context_out, kv_v, context_v, merged, sem,
):
    f32 = jnp.float32
    bf16 = jnp.bfloat16
    stores = [
        pltpu.make_async_copy(src, dst, sem.at[i])
        for i, (src, dst) in enumerate(
            ((new_w, w_out), (new_1, m1_out), (new_2, m2_out), (kv_v, kv_out), (context_v, context_out))
        )
    ]
    for store in stores[:3]:
        store.start()
    rows = kv_v.shape[0]
    token_rows = projected.shape[0]
    pad = query_rows.shape[0] // rows
    keys = projected[:, :HD]
    keys = keys * cosine[...] + pltpu.roll(keys, HD // 2, 1) * sine[...]
    values = projected[:, HD:]
    for row in range(rows):
        span = slice(row * STEPS, (row + 1) * STEPS)
        kv_v[row, :, :HD] = keys[span].astype(bf16)
        kv_v[row, :, HD:] = values[span].astype(bf16)
    stores[3].start()
    scores = lax.dot_general(
        query_rows[...], keys.astype(bf16), (((1,), (1,)), ((), ())), preferred_element_type=f32
    ) * SCORE_SCALE
    at = lax.broadcasted_iota(jnp.int32, scores.shape, 0)
    new = lax.broadcasted_iota(jnp.int32, scores.shape, 1)
    seen = (lax.div(at, pad) == lax.div(new, STEPS)) & (lax.rem(new, STEPS) <= lax.rem(at, STEPS))
    scores = jnp.where(seen, scores, masked_score)
    highest = jnp.maximum(jnp.max(scores, axis=-1, keepdims=True), top[...])
    exponent = jnp.exp(scores - highest[:, :token_rows])
    kept = jnp.exp(top[...] - highest)
    weight = kept * mass[...] + jnp.sum(exponent, axis=-1, keepdims=True)
    context = kept * cached[...] + jnp.dot(
        exponent.astype(bf16), values.astype(bf16), preferred_element_type=f32
    )
    merged[...] = (context / weight).reshape(merged.shape)
    for head in range(QH // KVH):
        context_v[:, :, pl.ds(head * HD, HD)] = merged[:, pl.ds(head * STEPS, STEPS)].astype(bf16)
    stores[4].start()
    for store in stores:
        store.wait()


def shards(
    sizes, tokens, queries, cache_keys, cache_values, lengths, weights, moment1, moment2, grad_parts
):
    nx, nz, nf, nt = sizes
    rows, columns = weights.shape
    row_count = tokens.shape[0]
    token_rows = row_count * STEPS
    span = cache_keys.shape[1]
    cx = columns // nx
    hc = columns // nt
    depth = nt * rows
    chunks = rows // CHUNK
    pad = 8 * pl.cdiv(STEPS * (QH // KVH), 8)
    dma = pltpu.SemaphoreType.DMA
    f32 = jnp.float32
    bf16 = jnp.bfloat16
    hbm = pl.BlockSpec(memory_space=pltpu.HBM)
    vmem = pl.BlockSpec(memory_space=pltpu.VMEM)
    shape = jax.ShapeDtypeStruct
    block = shape((rows, columns), f32)
    held = pl.pallas_call(
        functools.partial(exchange_kernel, nx, nz, nf, nt),
        out_shape=[block] * 3
        + [shape((token_rows, hc), f32), shape((row_count * pad, HD), bf16)]
        + [shape((row_count * pad, HD), f32)] * 3
        + [shape((token_rows, HD), f32)] * 2,
        in_specs=[hbm] * 9,
        out_specs=[vmem] * 10,
        scratch_shapes=[pltpu.VMEM((rows, columns), f32)] * 4
        + [
            pltpu.VMEM(tokens.shape, bf16),
            pltpu.VMEM(queries.shape, bf16),
            pltpu.VMEM(cache_keys.shape, bf16),
            pltpu.VMEM(cache_values.shape, bf16),
            pltpu.SMEM(lengths.shape, jnp.int32),
            pltpu.VMEM((token_rows, depth), f32),
            pltpu.VMEM((nf, token_rows, depth), bf16),
            pltpu.VMEM((row_count, pad, HD), f32),
            pltpu.VMEM((nx, rows, cx), bf16),
            pltpu.VMEM((nx - 1, rows, cx), bf16),
            pltpu.VMEM((nz, rows, cx), bf16),
            pltpu.VMEM((nx, rows, cx), bf16),
            pltpu.VMEM((nt, rows, hc), bf16),
            pltpu.VMEM((nt, rows, hc), bf16),
            pltpu.VMEM((nf, token_rows, depth), bf16),
            pltpu.VMEM((nf, token_rows, hc), f32),
            pltpu.VMEM((nf, token_rows, hc), bf16),
            pltpu.VMEM((nf, token_rows, hc), bf16),
            dma((chunks,)),
            dma((8,)),
        ]
        + [dma((chunks, nx - 1))] * 2
        + [dma((chunks, nz - 1))] * 2
        + [dma((chunks, nx - 1))] * 2
        + [dma((chunks, nt - 1))] * 2
        + [dma((nf - 1,))] * 4,
        compiler_params=pltpu.CompilerParams(
            collective_id=0, has_side_effects=True, vmem_limit_bytes=40 << 20
        ),
        name="exchange",
    )(
        *(
            pltpu.with_memory_space_constraint(operand, pltpu.HBM)
            for operand in (
                grad_parts, weights, moment1, moment2, tokens, queries, cache_keys, cache_values, lengths
            )
        )
    )
    return pl.pallas_call(
        finish_kernel,
        out_shape=[block] * 3
        + [shape((row_count, STEPS, hc), bf16), shape(queries.shape, bf16)],
        in_specs=[vmem] * 10,
        out_specs=[hbm] * 5,
        scratch_shapes=[
            pltpu.VMEM((row_count, STEPS, hc), bf16),
            pltpu.VMEM(queries.shape, bf16),
            pltpu.VMEM((row_count, pad, HD), f32),
            dma((5,)),
        ],
        compiler_params=pltpu.CompilerParams(vmem_limit_bytes=16 << 20),
        name="finish",
    )(*held)


def solution(mesh):
    in_specs = (
        P(("group", "fsdp"), None, None),
        P(("group", "fsdp"), None, "tp"),
        P(("group", "fsdp"), None, "tp"),
        P(("group", "fsdp"), None, "tp"),
        P(("group", "fsdp")),
        P(("fsdp", "tp"), None),
        P(("fsdp", "tp"), None),
        P(("fsdp", "tp"), None),
        P("group", ("fsdp", "tp"), None),
    )
    out_specs = (
        P(("fsdp", "tp"), None),
        P(("fsdp", "tp"), None),
        P(("fsdp", "tp"), None),
        P(("group", "fsdp"), None, "tp"),
        P(("group", "fsdp"), None, "tp"),
    )
    nx = X_CHIPS
    sizes = (nx, mesh.shape["group"] // nx, mesh.shape["fsdp"], mesh.shape["tp"])
    return jax.shard_map(
        functools.partial(shards, sizes),
        mesh=mesh,
        in_specs=in_specs,
        out_specs=out_specs,
        check_vma=False,
    )
```

time: 66.7 us -> 54.7 us (0.82)
  local copies, waits for them, and re-layouts: 11.3 us -> 0 us
  Pallas kernels: 52.1 us -> 54 us
  matrix products: 1.23 us -> 0 us
  other arithmetic: 0.95 us -> 0 us
    unnamed x21 -> x0, local copies, waits for them, and re-layouts: 9.4 us -> none
    pallas_call x1 -> x2, Pallas kernels: 52.1 us -> 54 us  [the longest x1 52.6 us: shards(): pl.pallas_call(functools.partial(exchange_kernel, nx, nz, nf, nt), out_sh...]
    dot_general x4 -> x0, matrix products: 1.23 us -> none  [the longest x1 0.54 us: shards(): jnp.einsum('risgd,rpsd->risgp', grouped, cached_keys, preferred_element_t...]
    reshape x2 -> x0, local copies, waits for them, and re-layouts: 1.16 us -> none  [the longest x1 1.14 us: shards(): token_rows = tokens.reshape(row_count * STEPS, tokens.shape[2])]
where the time goes in v2:
time: 54.7 us; the launch traced here: 54.6 us
  Pallas kernels  54 us (99%)
  between operations  0.64 us (1%)
    pallas_call x1, Pallas kernels, shards(): pl.pallas_call(functools.partial(exchange_kernel, nx, nz, nf, nt), out_sh...  52.6 us
    pallas_call x1, Pallas kernels, shards(): pl.pallas_call(finish_kernel, out_shape=[block] * 3 + [shape((row_count,...  1.32 us

profile of v2, /device:TPU:1, one launch (start us, length us, event | category | flops | bytes accessed | tf_op | source)
XLA Modules:
  0.0 54.6 jit_solution(13994024033638854605)
XLA Ops:
  0.6 52.6 %exchange.1 = (f32[80,2048]{1,0:T(8,128)S(1)}, f32[80,2048]{1,0:T(8,128)S(1)}, f32[80,2048]{1,0:T(8,128)S(1)}, f32[32,256]{1,0:T(8,128)S(1)}, bf16[192,128]{1,0:...) custom-call(f32[1,80,2048]{2,1,0:T(8,128)} %grad.1, ...), custom_call_target="tpu_custom_call" | custom-call | tf_op jit(solution)/shard_map/exchange/pallas_call | solution.py:326
  53.3 1.3 %finish.1 = (f32[80,2048]{1,0:T(8,128)}, f32[80,2048]{1,0:T(8,128)}, f32[80,2048]{1,0:T(8,128)}, bf16[8,4,256]{2,1,0:T(4,128)(2,1)}, bf16[8,4,640]{2,1,0:T(4,128)(2,1)}) custom-call(f32[80,2048]{1,0:T(8,128)S(1)} %get-tuple-element.15.new_w, f32[80,2048]{1,0:T(8,128)S(1)} %get-tuple-element.16.new_1, f32[80,2048]{1,0:T(8,128)S(1)} %get-tuple-element.17.new_2, ...), custom_call_target="tpu_custom_call" | custom-call | tf_op jit(solution)/shard_map/finish/pallas_call | solution.py:374

commit v3 on v2

--- a/solution.py
+++ b/solution.py
@@ -13,6 +13,7 @@
 HD = 128
 STEPS = 4
 X_CHIPS = 4
+SPAN = 1
 CHUNK = 16
 
 beta_one = 0.9
@@ -34,6 +35,14 @@
     direction = new_moment1 / correct_one / (jnp.sqrt(new_moment2 / correct_two) + epsilon)
     new_weights = weights - learning_rate * (direction + decay_rate * weights)
     return (new_weights, new_moment1, new_moment2)
+
+
+def flip(value, bits):
+    out = value
+    for b in range(bits.bit_length()):
+        if (bits >> b) % 2:
+            out = out + (1 << b) * (1 - 2 * lax.rem(lax.div(value, 1 << b), 2))
+    return out
 
 
 def exchange_kernel(
@@ -50,8 +59,8 @@
     x = lax.rem(group, nx)
     z = lax.div(group, nx)
     rows_all = grad_v.shape[0]
-    cx = gb.shape[2]
     hc = wf.shape[2]
+    hx = nt // nx
     depth = tall.shape[2]
     chunks = rows_all // CHUNK
     f32 = jnp.float32
@@ -59,18 +68,16 @@
 
     x_to = [z * nx + lax.rem(x + d, nx) for d in range(nx)]
     z_to = [lax.rem(z + d, nz) * nx + x for d in range(nz)]
-    f_at = [lax.rem(f + d, nf) for d in range(nf)]
+    f_by = [flip(f, k) for k in range(nf)]
     t_at = [lax.rem(t + d, nt) for d in range(nt)]
     x_from = [lax.rem(x + nx - d, nx) for d in range(nx)]
     z_from = [lax.rem(z + nz - d, nz) for d in range(nz)]
-    f_from = [lax.rem(f + nf - d, nf) for d in range(nf)]
-    t_from = [lax.rem(t + nt - d, nt) for d in range(nt)]
 
     barrier = pltpu.get_barrier_semaphore()
     peers = (
         [(z_to[d], f, t) for d in range(1, nz)]
         + [(group, f, t_at[d]) for d in range(1, nt)]
-        + [(group, f_at[d], t) for d in range(1, nf)]
+        + [(group, f_by[k], t) for k in range(1, nf)]
         + [(x_to[d], f, t) for d in range(1, nx)]
     )
     for peer in peers:
@@ -92,13 +99,13 @@
             )
         )
     ]
-    for load in loads + others:
+    for load in loads:
         load.start()
 
     def cast(r):
         loads[r].wait()
-        for i in range(nx):
-            gb[i, rows_of(r)] = grad_v[rows_of(r), pl.ds(i * cx, cx)].astype(bf16)
+        for h in range(nx * hx):
+            gb[h % nx, h // nx, rows_of(r)] = grad_v[rows_of(r), pl.ds(h * hc, hc)].astype(bf16)
 
     def remote(src, dst, send, recv, device):
         return pltpu.make_async_remote_copy(
@@ -116,63 +123,92 @@
     def arrive(dst, send_sem, recv_sem):
         remote(dst, dst, send_sem, recv_sem, (group, f, t)).wait_recv()
 
-    def scatter_x(r):
+    def part(at_x, r):
+        return lax.rem(at_x - r - t + nx * (chunks + nt), nx)
+
+    def scatter_x(u, r, es):
         for d in range(1, nx):
             send(
-                gb.at[lax.rem(x + d, nx), rows_of(r)], xr.at[d - 1, rows_of(r)],
-                xs.at[r, d - 1], xq.at[r, d - 1], (x_to[d], f, t),
+                gb.at[part(lax.rem(x + d, nx), r), es, rows_of(r)], xr.at[d - 1, es, rows_of(r)],
+                xs.at[u, d - 1], xq.at[u, d - 1], (x_to[d], f, t),
             )
 
-    def exchange_z(r):
-        total = gb[x, rows_of(r)].astype(f32)
+    def exchange_z(u, r, es):
+        total = gb[part(x, r), es, rows_of(r)].astype(f32)
         for d in range(1, nx):
-            arrive(xr.at[d - 1, rows_of(r)], xs.at[r, d - 1], xq.at[r, d - 1])
-            total += xr[d - 1, rows_of(r)].astype(f32)
-        zb[z, rows_of(r)] = total.astype(bf16)
+            arrive(xr.at[d - 1, es, rows_of(r)], xs.at[u, d - 1], xq.at[u, d - 1])
+            total += xr[d - 1, es, rows_of(r)].astype(f32)
+        zb[z, es, rows_of(r)] = total.astype(bf16)
+        piece = zb.at[z, es, rows_of(r)]
         for d in range(1, nz):
-            send(
-                zb.at[z, rows_of(r)], zb.at[z, rows_of(r)],
-                zs.at[r, d - 1], zq.at[r, d - 1], (z_to[d], f, t),
-            )
-
-    def gather_x(r):
+            send(piece, piece, zs.at[u, d - 1], zq.at[u, d - 1], (z_to[d], f, t))
+
+    def update(r, h, gradient):
+        columns = pl.ds(pl.multiple_of(h * hc, hc), hc)
+        w, one, two = adam_update(
+            w_v[rows_of(r), columns], m1_v[rows_of(r), columns], m2_v[rows_of(r), columns], gradient
+        )
+        new_w[rows_of(r), columns] = w
+        new_1[rows_of(r), columns] = one
+        new_2[rows_of(r), columns] = two
+        return w.astype(bf16)
+
+    to_heads = []
+
+    def own_part(u, r, es):
         for d in range(1, nz):
-            arrive(zb.at[z_from[d], rows_of(r)], zs.at[r, d - 1], zq.at[r, d - 1])
-        total = zb[0, rows_of(r)].astype(f32)
+            arrive(zb.at[z_from[d], es, rows_of(r)], zs.at[u, d - 1], zq.at[u, d - 1])
+        total = zb[0, es, rows_of(r)].astype(f32)
         for i in range(1, nz):
-            total += zb[i, rows_of(r)].astype(f32)
-        gf[x, rows_of(r)] = total.astype(bf16)
+            total += zb[i, es, rows_of(r)].astype(f32)
+        low = part(x, r)
+        rounded = total.astype(bf16)
+        gf[low, es, rows_of(r)] = rounded
+        for i in range(SPAN):
+            e = es.start + i
+            h = low + nx * e
+            wb[e, rows_of(r)] = update(r, h, rounded[i].astype(f32))
+            for d in x_order:
+                copy = remote(
+                    wb.at[e, rows_of(r)], wf.at[t, rows_of(r)],
+                    ys.at[r, e, d], yq.at[r, lax.div(t, nx), d], (x_to[d], f, h),
+                )
+                if d > 0:
+                    copy.start()
+                    started.append(copy)
+                else:
+                    pl.when(h != t)(copy.start)
+                    to_heads.append((h != t, copy))
+
+            @pl.when(h == t)
+            def _():
+                wf[t, rows_of(r)] = wb[e, rows_of(r)]
+
+    def collect(r):
+        for e in range(hx):
+            for d in range(nx):
+                source = part(x_from[d], r) + nx * e
+                piece = wf.at[source, rows_of(r)]
+                wait = remote(piece, piece, ys.at[r, e, d], yq.at[r, e, d], (group, f, t)).wait_recv
+                if d > 0:
+                    wait()
+                else:
+                    pl.when(source != t)(wait)
+
+    def gather_x(u, r, es):
+        piece = gf.at[part(x, r), es, rows_of(r)]
         for d in range(1, nx):
-            send(
-                gf.at[x, rows_of(r)], gf.at[x, rows_of(r)],
-                gs.at[r, d - 1], gq.at[r, d - 1], (x_to[d], f, t),
-            )
-
-    t_order = sorted(range(1, nt), key=lambda d: -min(d, nt - d))
-
-    def update(r):
+            send(piece, piece, gs.at[u, d - 1], gq.at[u, d - 1], (x_to[d], f, t))
+
+    def other_parts(u, r, es):
         for d in range(1, nx):
-            arrive(gf.at[x_from[d], rows_of(r)], gs.at[r, d - 1], gq.at[r, d - 1])
-        for i in range(nx):
-            columns = pl.ds(i * cx, cx)
-            w, one, two = adam_update(
-                w_v[rows_of(r), columns],
-                m1_v[rows_of(r), columns],
-                m2_v[rows_of(r), columns],
-                gf[i, rows_of(r)].astype(f32),
-            )
-            new_w[rows_of(r), columns] = w
-            new_1[rows_of(r), columns] = one
-            new_2[rows_of(r), columns] = two
-            rounded = w.astype(bf16)
-            for j in range(cx // hc):
-                wb[i * (cx // hc) + j, rows_of(r)] = rounded[:, j * hc : (j + 1) * hc]
-        for d in t_order:
-            send(
-                wb.at[t_at[d], rows_of(r)], wf.at[t, rows_of(r)],
-                ys.at[r, d - 1], yq.at[r, d - 1], (group, f, t_at[d]),
-            )
-        wf[t, rows_of(r)] = wb[t, rows_of(r)]
+            low = part(x_from[d], r)
+            arrive(gf.at[low, es, rows_of(r)], gs.at[u, d - 1], gq.at[u, d - 1])
+            for i in range(SPAN):
+                e = es.start + i
+                update(r, low + nx * e, gf[low, e, rows_of(r)].astype(f32))
+
+    x_order = sorted(range(nx), key=lambda d: -min(d, nx - d))
 
     def lay_out_tokens():
         others[0].wait()
@@ -216,44 +252,56 @@
         turn = jnp.sin(angle)
         sine[...] = jnp.where(lane < HD // 2, -turn, turn)
 
-    for r in range(chunks):
-        cast(r)
+    spans = range(0, hx, SPAN)
+    units = [
+        (r * len(spans) + i, r, pl.ds(e, SPAN)) for r in range(chunks) for i, e in enumerate(spans)
+    ]
+    per_chunk = len(spans)
+    cast(0)
     pl.semaphore_wait(barrier, len(peers))
     for r in range(chunks):
-        scatter_x(r)
+        if r > 0:
+            cast(r)
+        for unit in units[r * per_chunk : (r + 1) * per_chunk]:
+            scatter_x(*unit)
+    for load in others:
+        load.start()
+    for unit in units:
+        exchange_z(*unit)
     lay_out_tokens()
-    attend_cache()
-    for r in range(chunks):
-        exchange_z(r)
-    for d in range(1, nf):
-        send(tb.at[f_at[d]], tall.at[f], ts.at[d - 1], tq.at[d - 1], (group, f_at[d], t))
+    f_order = sorted(range(1, nf), key=lambda k: -(k // 2))
+    for k in f_order:
+        send(tb.at[f_by[k]], tall.at[f], ts.at[k - 1], tq.at[k - 1], (group, f_by[k], t))
     for load in others[5:]:
         load.wait()
-    gather_x(0)
-    for r in range(1, chunks):
-        gather_x(r)
-        update(r - 1)
-    update(chunks - 1)
-
-    for d in range(1, nf):
-        arrive(tall.at[f_from[d]], ts.at[d - 1], tq.at[d - 1])
+    for unit in units:
+        own_part(*unit)
+    for unit in units:
+        gather_x(*unit)
+
+    for k in f_order:
+        arrive(tall.at[f_by[k]], ts.at[k - 1], tq.at[k - 1])
     for r in range(chunks):
-        for d in range(1, nt):
-            arrive(wf.at[t_from[d], rows_of(r)], ys.at[r, d - 1], yq.at[r, d - 1])
+        collect(r)
     partial = jnp.dot(
         tall[...].reshape(-1, depth), wf[...].reshape(depth, hc), preferred_element_type=f32
     ).reshape(pf.shape)
     pb[...] = partial.astype(bf16)
-    for d in range(1, nf):
-        send(pb.at[f_at[d]], pr.at[f], ps.at[d - 1], pq.at[d - 1], (group, f_at[d], t))
+    for k in f_order:
+        send(pb.at[f_by[k]], pr.at[f], ps.at[k - 1], pq.at[k - 1], (group, f_by[k], t))
     pf[...] = partial
+    attend_cache()
+    for unit in units:
+        other_parts(*unit)
     total = pf[f]
-    for d in range(1, nf):
-        arrive(pr.at[f_from[d]], ps.at[d - 1], pq.at[d - 1])
-        total += pr[f_from[d]].astype(f32)
+    for k in f_order:
+        arrive(pr.at[f_by[k]], ps.at[k - 1], pq.at[k - 1])
+        total += pr[f_by[k]].astype(f32)
     projected[...] = total
     for copy in started:
         copy.wait_send()
+    for apart, copy in to_heads:
+        pl.when(apart)(copy.wait_send)
 
 
 def finish_kernel(
@@ -311,7 +359,7 @@
     row_count = tokens.shape[0]
     token_rows = row_count * STEPS
     span = cache_keys.shape[1]
-    cx = columns // nx
+    hx = nt // nx
     hc = columns // nt
     depth = nt * rows
     chunks = rows // CHUNK
@@ -341,11 +389,11 @@
             pltpu.VMEM((token_rows, depth), f32),
             pltpu.VMEM((nf, token_rows, depth), bf16),
             pltpu.VMEM((row_count, pad, HD), f32),
-            pltpu.VMEM((nx, rows, cx), bf16),
-            pltpu.VMEM((nx - 1, rows, cx), bf16),
-            pltpu.VMEM((nz, rows, cx), bf16),
-            pltpu.VMEM((nx, rows, cx), bf16),
-            pltpu.VMEM((nt, rows, hc), bf16),
+            pltpu.VMEM((nx, hx, rows, hc), bf16),
+            pltpu.VMEM((nx - 1, hx, rows, hc), bf16),
+            pltpu.VMEM((nz, hx, rows, hc), bf16),
+            pltpu.VMEM((nx, hx, rows, hc), bf16),
+            pltpu.VMEM((hx, rows, hc), bf16),
             pltpu.VMEM((nt, rows, hc), bf16),
             pltpu.VMEM((nf, token_rows, depth), bf16),
             pltpu.VMEM((nf, token_rows, hc), f32),
@@ -354,10 +402,10 @@
             dma((chunks,)),
             dma((8,)),
         ]
-        + [dma((chunks, nx - 1))] * 2
-        + [dma((chunks, nz - 1))] * 2
-        + [dma((chunks, nx - 1))] * 2
-        + [dma((chunks, nt - 1))] * 2
+        + [dma((chunks * hx // SPAN, nx - 1))] * 2
+        + [dma((chunks * hx // SPAN, nz - 1))] * 2
+        + [dma((chunks * hx // SPAN, nx - 1))] * 2
+        + [dma((chunks, hx, nx))] * 2
         + [dma((nf - 1,))] * 4,
         compiler_params=pltpu.CompilerParams(
             collective_id=0, has_side_effects=True, vmem_limit_bytes=40 << 20

time: 54.7 us -> 49.5 us (0.905)
  Pallas kernels: 54 us -> 48.7 us
    pallas_call x1, Pallas kernels: 52.6 us -> 47.4 us  [shards(): pl.pallas_call(functools.partial(exchange_kernel, nx, nz, nf, nt), out_sh...]
where the time goes in v3:
time: 49.5 us; the launch traced here: 49.4 us
  Pallas kernels  48.7 us (98%)
  between operations  0.64 us (1%)
    pallas_call x1, Pallas kernels, shards(): pl.pallas_call(functools.partial(exchange_kernel, nx, nz, nf, nt), out_sh...  47.4 us
    pallas_call x1, Pallas kernels, shards(): pl.pallas_call(finish_kernel, out_shape=[block] * 3 + [shape((row_count,...  1.32 us

profile of v3, /device:TPU:1, one launch (start us, length us, event | category | flops | bytes accessed | tf_op | source)
XLA Modules:
  0.0 49.4 jit_solution(14607249952468310703)
XLA Ops:
  0.6 47.4 %exchange.1 = (f32[80,2048]{1,0:T(8,128)S(1)}, f32[80,2048]{1,0:T(8,128)S(1)}, f32[80,2048]{1,0:T(8,128)S(1)}, f32[32,256]{1,0:T(8,128)S(1)}, bf16[192,128]{1,0:...) custom-call(f32[1,80,2048]{2,1,0:T(8,128)} %grad.1, ...), custom_call_target="tpu_custom_call" | custom-call | tf_op jit(solution)/shard_map/exchange/pallas_call | solution.py:374
  48.1 1.3 %finish.1 = (f32[80,2048]{1,0:T(8,128)}, f32[80,2048]{1,0:T(8,128)}, f32[80,2048]{1,0:T(8,128)}, bf16[8,4,256]{2,1,0:T(4,128)(2,1)}, bf16[8,4,640]{2,1,0:T(4,128)(2,1)}) custom-call(f32[80,2048]{1,0:T(8,128)S(1)} %get-tuple-element.15.new_w, f32[80,2048]{1,0:T(8,128)S(1)} %get-tuple-element.16.new_1, f32[80,2048]{1,0:T(8,128)S(1)} %get-tuple-element.17.new_2, ...), custom_call_target="tpu_custom_call" | custom-call | tf_op jit(solution)/shard_map/finish/pallas_call | solution.py:422

commit v4 on v3

--- a/solution.py
+++ b/solution.py
@@ -32,7 +32,7 @@
 def adam_update(weights, moment1, moment2, gradient):
     new_moment1 = beta_one * moment1 + (1.0 - beta_one) * gradient
     new_moment2 = beta_two * moment2 + (1.0 - beta_two) * gradient * gradient
-    direction = new_moment1 / correct_one / (jnp.sqrt(new_moment2 / correct_two) + epsilon)
+    direction = new_moment1 * (1.0 / correct_one) / (jnp.sqrt(new_moment2 * (1.0 / correct_two)) + epsilon)
     new_weights = weights - learning_rate * (direction + decay_rate * weights)
     return (new_weights, new_moment1, new_moment2)
 
@@ -270,11 +270,13 @@
         exchange_z(*unit)
     lay_out_tokens()
     f_order = sorted(range(1, nf), key=lambda k: -(k // 2))
+    for load in others[5:]:
+        load.wait()
+    for unit in units[:4]:
+        own_part(*unit)
     for k in f_order:
         send(tb.at[f_by[k]], tall.at[f], ts.at[k - 1], tq.at[k - 1], (group, f_by[k], t))
-    for load in others[5:]:
-        load.wait()
-    for unit in units:
+    for unit in units[4:]:
         own_part(*unit)
     for unit in units:
         gather_x(*unit)

time: 49.5 us -> 48 us (0.970)
  Pallas kernels: 48.7 us -> 47.2 us
    pallas_call x1, Pallas kernels: 47.4 us -> 45.9 us  [shards(): pl.pallas_call(functools.partial(exchange_kernel, nx, nz, nf, nt), out_sh...]
where the time goes in v4:
time: 48 us; the launch traced here: 47.8 us
  Pallas kernels  47.2 us (98%)
  between operations  0.64 us (1%)
    pallas_call x1, Pallas kernels, shards(): pl.pallas_call(functools.partial(exchange_kernel, nx, nz, nf, nt), out_sh...  45.9 us
    pallas_call x1, Pallas kernels, shards(): pl.pallas_call(finish_kernel, out_shape=[block] * 3 + [shape((row_count,...  1.32 us

profile of v4, /device:TPU:1, one launch (start us, length us, event | category | flops | bytes accessed | tf_op | source)
XLA Modules:
  0.0 47.8 jit_solution(50593337206239818)
XLA Ops:
  0.6 45.9 %exchange.1 = (f32[80,2048]{1,0:T(8,128)S(1)}, f32[80,2048]{1,0:T(8,128)S(1)}, f32[80,2048]{1,0:T(8,128)S(1)}, f32[32,256]{1,0:T(8,128)S(1)}, bf16[192,128]{1,0:...) custom-call(f32[1,80,2048]{2,1,0:T(8,128)} %grad.1, ...), custom_call_target="tpu_custom_call" | custom-call | tf_op jit(solution)/shard_map/exchange/pallas_call | solution.py:376
  46.5 1.3 %finish.1 = (f32[80,2048]{1,0:T(8,128)}, f32[80,2048]{1,0:T(8,128)}, f32[80,2048]{1,0:T(8,128)}, bf16[8,4,256]{2,1,0:T(4,128)(2,1)}, bf16[8,4,640]{2,1,0:T(4,128)(2,1)}) custom-call(f32[80,2048]{1,0:T(8,128)S(1)} %get-tuple-element.15.new_w, f32[80,2048]{1,0:T(8,128)S(1)} %get-tuple-element.16.new_1, f32[80,2048]{1,0:T(8,128)S(1)} %get-tuple-element.17.new_2, ...), custom_call_target="tpu_custom_call" | custom-call | tf_op jit(solution)/shard_map/finish/pallas_call | solution.py:424

commit v5 on v4

--- a/solution.py
+++ b/solution.py
@@ -51,7 +51,7 @@
     new_w, new_1, new_2, projected, query_rows, top, mass, cached, cosine, sine,
     grad_v, w_v, m1_v, m2_v, tok_v, q_v, k_v, v_v, len_s, row_v, tb, qf,
     gb, xr, zb, gf, wb, wf, tall, pf, pb, pr,
-    grad_sem, in_sem, xs, xq, zs, zq, gs, gq, ys, yq, ts, tq, ps, pq,
+    go_z, go_t, go_f, grad_sem, in_sem, xs, xq, zs, zq, gs, gq, ys, yq, ts, tq, ps, pq,
 ):
     group = lax.axis_index("group")
     f = lax.axis_index("fsdp")
@@ -73,15 +73,29 @@
     x_from = [lax.rem(x + nx - d, nx) for d in range(nx)]
     z_from = [lax.rem(z + nz - d, nz) for d in range(nz)]
 
+    def place(at_t):
+        return jnp.where(at_t > nt // 2, 2 * (nt - at_t), jnp.maximum(2 * at_t - 1, 0))
+
+    rank = place(t)
+    peers = (
+        [((z_to[d], f, t), z + d < nz, go_z.at[nz - d - 1]) for d in range(1, nz)]
+        + [((group, f, t_at[d]), place(t_at[d]) > rank, go_t) for d in range(1, nt)]
+        + [((group, f_by[k], t), f_by[k] > f, go_f) for k in range(1, nf)]
+    )
     barrier = pltpu.get_barrier_semaphore()
-    peers = (
-        [(z_to[d], f, t) for d in range(1, nz)]
-        + [(group, f, t_at[d]) for d in range(1, nt)]
-        + [(group, f_by[k], t) for k in range(1, nf)]
-        + [(x_to[d], f, t) for d in range(1, nx)]
-    )
-    for peer in peers:
-        pl.semaphore_signal(barrier, inc=1, device_id=peer, device_id_type=MESH)
+
+    def greet(semaphore, device):
+        pl.semaphore_signal(semaphore, inc=1, device_id=device, device_id_type=MESH)
+
+    for d in range(1, nx):
+        greet(barrier, (x_to[d], f, t))
+    for device, later, _ in peers:
+        pl.when(later)(functools.partial(greet, barrier, device))
+
+    def answer():
+        pl.semaphore_wait(barrier, nx - 1 + z + rank + f)
+        for device, later, go in peers:
+            pl.when(jnp.logical_not(later))(functools.partial(greet, go, device))
 
     def rows_of(r):
         return pl.ds(r * CHUNK, CHUNK)
@@ -139,9 +153,19 @@
             arrive(xr.at[d - 1, es, rows_of(r)], xs.at[u, d - 1], xq.at[u, d - 1])
             total += xr[d - 1, es, rows_of(r)].astype(f32)
         zb[z, es, rows_of(r)] = total.astype(bf16)
+        for d in range(1, nz):
+            pl.when(z + d >= nz)(z_copy(d, u, r, es).start)
+
+    def z_copy(d, u, r, es):
         piece = zb.at[z, es, rows_of(r)]
-        for d in range(1, nz):
-            send(piece, piece, zs.at[u, d - 1], zq.at[u, d - 1], (z_to[d], f, t))
+        return remote(piece, piece, zs.at[u, d - 1], zq.at[u, d - 1], (z_to[d], f, t))
+
+    def exchange_z_later(d):
+        @pl.when(z + d < nz)
+        def _():
+            pl.semaphore_wait(go_z.at[d - 1], 1)
+            for unit in units:
+                z_copy(d, *unit).start()
 
     def update(r, h, gradient):
         columns = pl.ds(pl.multiple_of(h * hc, hc), hc)
@@ -258,7 +282,7 @@
     ]
     per_chunk = len(spans)
     cast(0)
-    pl.semaphore_wait(barrier, len(peers))
+    answer()
     for r in range(chunks):
         if r > 0:
             cast(r)
@@ -269,9 +293,21 @@
     for unit in units:
         exchange_z(*unit)
     lay_out_tokens()
+
+    @pl.when(f < nf - 1)
+    def _():
+        pl.semaphore_wait(go_f, nf - 1 - f)
+
     f_order = sorted(range(1, nf), key=lambda k: -(k // 2))
+    for d in range(1, nz):
+        exchange_z_later(d)
     for load in others[5:]:
         load.wait()
+
+    @pl.when(rank < nt - 1)
+    def _():
+        pl.semaphore_wait(go_t, nt - 1 - rank)
+
     for unit in units[:4]:
         own_part(*unit)
     for k in f_order:
@@ -302,6 +338,9 @@
     projected[...] = total
     for copy in started:
         copy.wait_send()
+    for d in range(1, nz):
+        for unit in units:
+            z_copy(d, *unit).wait_send()
     for apart, copy in to_heads:
         pl.when(apart)(copy.wait_send)
 
@@ -401,6 +440,9 @@
             pltpu.VMEM((nf, token_rows, hc), f32),
             pltpu.VMEM((nf, token_rows, hc), bf16),
             pltpu.VMEM((nf, token_rows, hc), bf16),
+            pltpu.SemaphoreType.REGULAR((nz - 1,)),
+            pltpu.SemaphoreType.REGULAR,
+            pltpu.SemaphoreType.REGULAR,
             dma((chunks,)),
             dma((8,)),
         ]

time: 48 us -> 48.6 us (1.012)
  Pallas kernels: 47.2 us -> 47.8 us
    pallas_call x1, Pallas kernels: 45.9 us -> 46.5 us  [shards(): pl.pallas_call(functools.partial(exchange_kernel, nx, nz, nf, nt), out_sh...]
where the time goes in v5:
time: 48.6 us; the launch traced here: 48.5 us
  Pallas kernels  47.8 us (98%)
  between operations  0.64 us (1%)
    pallas_call x1, Pallas kernels, shards(): pl.pallas_call(functools.partial(exchange_kernel, nx, nz, nf, nt), out_sh...  46.5 us
    pallas_call x1, Pallas kernels, shards(): pl.pallas_call(finish_kernel, out_shape=[block] * 3 + [shape((row_count,...  1.32 us

profile of v5, /device:TPU:1, one launch (start us, length us, event | category | flops | bytes accessed | tf_op | source)
XLA Modules:
  0.0 48.5 jit_solution(11864552497239343546)
XLA Ops:
  0.6 46.5 %exchange.1 = (f32[80,2048]{1,0:T(8,128)S(1)}, f32[80,2048]{1,0:T(8,128)S(1)}, f32[80,2048]{1,0:T(8,128)S(1)}, f32[32,256]{1,0:T(8,128)S(1)}, bf16[192,128]{1,0:...) custom-call(f32[1,80,2048]{2,1,0:T(8,128)} %grad.1, ...), custom_call_target="tpu_custom_call" | custom-call | tf_op jit(solution)/shard_map/exchange/pallas_call | solution.py:415
  47.1 1.3 %finish.1 = (f32[80,2048]{1,0:T(8,128)}, f32[80,2048]{1,0:T(8,128)}, f32[80,2048]{1,0:T(8,128)}, bf16[8,4,256]{2,1,0:T(4,128)(2,1)}, bf16[8,4,640]{2,1,0:T(4,128)(2,1)}) custom-call(f32[80,2048]{1,0:T(8,128)S(1)} %get-tuple-element.15.new_w, f32[80,2048]{1,0:T(8,128)S(1)} %get-tuple-element.16.new_1, f32[80,2048]{1,0:T(8,128)S(1)} %get-tuple-element.17.new_2, ...), custom_call_target="tpu_custom_call" | custom-call | tf_op jit(solution)/shard_map/finish/pallas_call | solution.py:466
